TPU v7x, 256 devices: a whole 4x4x8 slice. The times are simulated.
256 devices in a mesh: grid: 32 (over z, y), var: 8 (over x, core).
Axes of the slice: x: 4, y: 4, z: 8, core: 2. Of those that a mesh axis runs over, the one named last changes fastest.
Arguments:
- data: bfloat16 [8, 1024, 49152], P('var', None, 'grid'), may hold values from -6 to 6
- area: float32 [49152], P('grid'), may hold values from 0.1 to 1
- eofs: bfloat16 [8, 49152, 128], P('var', 'grid'), may hold values from -0.02734375 to 0.02734375
- var_scale: float32 [8], P('var'), may hold values from 0.5 to 2
- recon_map: bfloat16 [8, 1024, 49152], P('var', None, 'grid'), may hold values from -0.1875 to 0.1875
Outputs:
- fields: bfloat16 [8, 1024, 49152], P('var', None, 'grid')
All inputs are finite; a program needn't handle non-finite values.
Results may differ from a plain program's by a relative error of at most 0.0057.
Values may be sent and summed in bfloat16 or wider, within the bound.
No kernel may reach another device: no remote copies, remote signals or barrier semaphores. Data moves between devices by JAX's collectives and lax.ppermute only.
A program may use at most 64 MiB of HBM per device.

v0:
```python
import jax
import jax.numpy as jnp
from jax import lax
from jax.sharding import PartitionSpec as P


def body(data, area, eofs, var_scale, recon_map):
    scaled = (area[:, None] * eofs[0].astype(jnp.float32)).astype(jnp.bfloat16)
    partial_comps = jnp.dot(data[0], scaled, preferred_element_type=jnp.float32)
    comps = lax.psum(partial_comps, "grid")
    joined_local = (var_scale[0] * comps).astype(jnp.bfloat16)
    patterns = recon_map[0]
    rebuilt = jnp.dot(
        lax.all_gather(joined_local, "var", axis=1, tiled=True),
        patterns,
        preferred_element_type=jnp.float32,
    )
    return rebuilt.astype(jnp.bfloat16)[None]


def solution(mesh):
    placed = (
        P("var", None, "grid"),
        P("grid"),
        P("var", "grid", None),
        P("var"),
        P("var", None, "grid"),
    )
    return jax.shard_map(
        body, mesh=mesh, in_specs=placed, out_specs=P("var", None, "grid"), check_vma=False
    )
```

profile of v0, /device:TPU:1, one launch (start us, length us, event | category | flops | bytes accessed | tf_op | source)
XLA Modules:
  0.0 204.4 jit_solution(12069375334948118248)
XLA Ops:
  6.5 0.0 copy-start
  6.5 0.0 all-reduce.2.cloned.1.call-start
  6.5 4.0 %fusion.4 = f32[1024,128]{1,0:T(8,128)} fusion(bf16[1,1024,1536]{2,1,0:T(8,128)(2,1)} %param.5, bf16[1,1536,128]{2,1,0:T(8,128)(2,1)} %param.7, f32[1536]{0:T(1024)} %param.6), kind=kOutput, calls=%fused_computation.5 | convolution fusion | flops 403243008 | bytes 4069376 | tf_op jit(solution)/shard_map/dot_general | solution.py:9
  10.6 0.0 all-reduce.2.cloned.1.call-update
  10.6 0.0 all-gather.2.cloned.1.call-start
  11.3 146.2 %all-reduce.2.cloned.1.call-done = f32[1024,128]{1,0:T(8,128)} async-done(((f32[1024,128]{1,0:T(8,128)}), f32[1024,128]{1,0:T(8,128)}) %all-reduce.2.cloned.1.call-update) | async-done | bytes 524304 | tf_op jit(solution)/shard_map/psum | solution.py:10
  157.5 1.8 multiply_convert_fusion.1
  159.3 0.0 all-gather.2.cloned.1.call-update
  159.3 31.9 %all-gather.2.cloned.1.call-done = bf16[1024,1024]{1,0:T(8,128)(2,1)} async-done(((bf16[1024,128]{1,0:T(8,128)(2,1)}), bf16[1024,1024]{1,0:T(8,128)(2,1)}) %all-gather.2.cloned.1.call-update) | async-done | bytes 2097168 | tf_op jit(solution)/shard_map/all_gather | solution.py:14
  191.2 0.0 copy-done
  191.2 6.3 %fusion = bf16[1,1024,1536]{2,1,0:T(8,128)(2,1)} fusion(bf16[1024,1024]{1,0:T(8,128)(2,1)} %all-gather.2.cloned.1.call-done, bf16[1,1024,1536]{2,1,0:T(8,128)(2,1)S(1)} %copy-done), kind=kOutput, calls=%fused_computation.1 | convolution fusion | flops 3222798336 | bytes 8388608 | tf_op jit(solution)/shard_map/dot_general | solution.py:13
Async XLA Ops:
  6.5 184.7 %copy-start = (bf16[1,1024,1536]{2,1,0:T(8,128)(2,1)S(1)}, bf16[1,1024,1536]{2,1,0:T(8,128)(2,1)}, u32[]{:S(2)}) copy-start(bf16[1,1024,1536]{2,1,0:T(8,128)(2,1)} %param.9) | copy-start | bytes 9437188
  6.5 151.0 %all-reduce.2.cloned.1.call-start = ((), (), s32[]{:S(2)}) async-start(), calls=%async_computation | async-start | bytes 1048576 | tf_op jit(solution)/shard_map/psum | solution.py:10
  10.6 180.6 %all-gather.2.cloned.1.call-start = ((), (), s32[]{:S(2)}) async-start(), calls=%async_computation.1 | async-start | bytes 2359296 | tf_op jit(solution)/shard_map/all_gather | solution.py:14
Sparse Core Ops, SparseCore 0:
  10.8 146.7 all-reduce.1
  159.5 31.6 all-gather.1
where the time goes:
time: 205 us; the launch traced here: 204 us
  waiting for transfers between devices  178 us (87%)
  between operations  14 us (7%)
  matrix products  10.4 us (5%)
    psum x1, waiting for transfers between devices, body(): comps = lax.psum(partial_comps, 'grid')  146 us
    all_gather x1, waiting for transfers between devices, body(): lax.all_gather(joined_local, 'var', axis=1, tiled=True)  31.9 us
    dot_general x1, matrix products, body(): jnp.dot(lax.all_gather(joined_local, 'var', axis=1, tiled=True), patterns...  6.35 us
  transfers between devices with their start and end apart: 2, of which 2 were waited for; matrix products, arithmetic and copies ran while one was open for 0% of the time, Pallas kernels for 0%

commit v1 on v0

v1 whole, which is shorter than its diff:
```python
import jax
import jax.numpy as jnp
from jax import lax
from jax.sharding import Mesh, PartitionSpec as P

GRID = ("z", "y")


def gather(block, axes, count):
    spread = jnp.broadcast_to(block[None], (count, *block.shape))
    return lax.all_to_all(spread, axes, 0, 0, tiled=True)


def body(data, area, eofs, var_scale, recon_map):
    scaled = (area[:, None] * eofs[0].astype(jnp.float32)).astype(jnp.bfloat16)
    partial_comps = jnp.dot(data[0], scaled, preferred_element_type=jnp.float32)
    steps, modes = partial_comps.shape
    points = lax.axis_size("z") * lax.axis_size("y")
    pieces = partial_comps.astype(jnp.bfloat16).reshape(points, steps // points, modes)
    pieces = lax.all_to_all(pieces, GRID, 0, 0, tiled=True)
    comps = jnp.sum(pieces.astype(jnp.float32), axis=0)
    own = (var_scale[0] * comps).astype(jnp.bfloat16)
    mine = gather(own, GRID, points).reshape(steps, modes)
    across = gather(mine, "x", lax.axis_size("x"))
    other = lax.ppermute(across, "c", [(0, 1), (1, 0)])
    first = lax.axis_index("c") == 0
    both = jnp.stack([jnp.where(first, across, other), jnp.where(first, other, across)])
    joined = jnp.transpose(both, (2, 1, 0, 3)).reshape(steps, -1)
    rebuilt = jnp.dot(joined, recon_map[0], preferred_element_type=jnp.float32)
    return rebuilt.astype(jnp.bfloat16)[None]


def solution(mesh):
    fine = Mesh(mesh.devices.reshape(8, 4, 4, 2), ("z", "y", "x", "c"))
    var = ("x", "c")
    placed = (
        P(var, None, GRID),
        P(GRID),
        P(var, GRID, None),
        P(var),
        P(var, None, GRID),
    )
    return jax.shard_map(
        body, mesh=fine, in_specs=placed, out_specs=P(var, None, GRID), check_vma=False
    )
```

time: 205 us -> 73.9 us (0.36)
  waiting for transfers between devices: 178 us -> 13.2 us
  blocking collectives: 0 us -> 29.8 us
  starting transfers between devices: 0.04 us -> 17.3 us
  between operations: 14 us -> 0.72 us
  local copies, waits for them, and re-layouts: 0.01 us -> 2.08 us
    psum x1 -> x0, waiting for transfers between devices: 146 us -> none  [body(): comps = lax.psum(partial_comps, 'grid')]
    all_gather x1 -> x0, waiting for transfers between devices: 31.9 us -> none  [body(): lax.all_gather(joined_local, 'var', axis=1, tiled=True)]
    all_to_all x0 -> x2, blocking collectives: none -> 29.8 us  [gather(): return lax.all_to_all(spread, axes, 0, 0, tiled=True)]
    all_to_all x0 -> x1, starting transfers between devices: none -> 12 us  [body(): pieces = lax.all_to_all(pieces, GRID, 0, 0, tiled=True)]
    all_to_all x0 -> x1, waiting for transfers between devices: none -> 10.5 us  [body(): pieces = lax.all_to_all(pieces, GRID, 0, 0, tiled=True)]
    ppermute x0 -> x1, starting transfers between devices: none -> 5.26 us  [body(): other = lax.ppermute(across, 'c', [(0, 1), (1, 0)])]
    ppermute x0 -> x1, waiting for transfers between devices: none -> 2.63 us  [body(): other = lax.ppermute(across, 'c', [(0, 1), (1, 0)])]
where the time goes in v1:
time: 73.9 us; the launch traced here: 73.6 us
  blocking collectives  29.8 us (40%)
  starting transfers between devices  17.3 us (23%)
  waiting for transfers between devices  13.2 us (18%)
  matrix products  8.61 us (12%)
  local copies, waits for them, and re-layouts  2.08 us (3%)
  other arithmetic  1.93 us (3%)
    all_to_all x2, blocking collectives, gather(): return lax.all_to_all(spread, axes, 0, 0, tiled=True)  29.8 us
    all_to_all x1, starting transfers between devices, body(): pieces = lax.all_to_all(pieces, GRID, 0, 0, tiled=True)  12 us
    all_to_all x1, waiting for transfers between devices, body(): pieces = lax.all_to_all(pieces, GRID, 0, 0, tiled=True)  10.5 us
    ppermute x1, starting transfers between devices, body(): other = lax.ppermute(across, 'c', [(0, 1), (1, 0)])  5.26 us
    dot_general x1, matrix products, body(): rebuilt = jnp.dot(joined, recon_map[0], preferred_element_type=jnp.float32)  4.94 us
    dot_general x1, matrix products, body(): partial_comps = jnp.dot(data[0], scaled, preferred_element_type=jnp.float32)  3.67 us
    ppermute x1, waiting for transfers between devices, body(): other = lax.ppermute(across, 'c', [(0, 1), (1, 0)])  2.63 us
    another operation x2, other arithmetic, body(): jnp.stack([jnp.where(first, across, other), jnp.where(first, other, acros...  1.87 us
  transfers between devices with their start and end apart: 2, of which 2 were waited for; matrix products, arithmetic and copies ran while one was open for 0% of the time, Pallas kernels for 0%

profile of v1, /device:TPU:1, one launch (start us, length us, event | category | flops | bytes accessed | tf_op | source)
XLA Modules:
  0.0 73.6 jit_solution(11450839504385822510)
XLA Ops:
  0.0 0.0 copy-start
  0.0 3.7 %fusion.7 = bf16[1024,128]{0,1:T(8,128)(2,1)S(1)} fusion(bf16[1,1024,1536]{2,1,0:T(8,128)(2,1)} %param.5, bf16[1,1536,128]{2,1,0:T(8,128)(2,1)} %param.7, f32[1536]{0:T(1024)} %param.6), kind=kOutput, calls=%fused_computation.7 | convolution fusion | flops 403374080 | bytes 3807232 | tf_op jit(solution)/shard_map/dot_general | solution.py:16
  3.7 0.8 %copy.8 = bf16[1024,128]{1,0:T(8,128)(2,1)} copy(bf16[1024,128]{0,1:T(8,128)(2,1)S(1)} %fusion.7) | data formatting | bytes 524288 | tf_op jit(solution)/shard_map/convert_element_type | solution.py:19
  4.5 12.0 %all-to-all-start = ((bf16[32,32,128]{2,1,0:T(8,128)(2,1)}), bf16[32,32,128]{2,1,0:T(8,128)(2,1)S(1)}, u32[]{:S(2)}, u32[]{:S(2)}) async-start(bf16[32,32,128]{2,1,0:T(8,128)(2,1)} %bitcast.32), calls=%async_computation | async-start | bytes 524288 | tf_op jit(solution)/shard_map/all_to_all | solution.py:20
  17.2 10.5 %all-to-all-done = bf16[32,32,128]{2,1,0:T(8,128)(2,1)S(1)} async-done(((bf16[32,32,128]{2,1,0:T(8,128)(2,1)}), bf16[32,32,128]{2,1,0:T(8,128)(2,1)S(1)}, u32[]{:S(2)}, u32[]{:S(2)}) %all-to-all-start) | async-done | bytes 262176 | tf_op jit(solution)/shard_map/all_to_all | solution.py:20
  27.9 15.1 %all_to_all.15 = bf16[32,32,128]{2,1,0:T(8,128)(2,1)} all-to-all(bf16[32,32,128]{2,1,0:T(8,128)(2,1)S(1)} %broadcast_in_dim.8), channel_id=1, replica_groups=mesh['z'=8,'y'=4,'x'=4,'c'=2] {'z','y'}, dimensions={0} | all-to-all | bytes 524288 | tf_op jit(solution)/shard_map/all_to_all | solution.py:11
  42.9 1.1 %copy.9 = bf16[1024,128]{0,1:T(8,128)(2,1)S(1)} copy(bf16[1024,128]{1,0:T(8,128)(2,1)} %bitcast.33) | data formatting | bytes 524288 | tf_op jit(solution)/shard_map/broadcast_in_dim | solution.py:10
  44.0 0.1 broadcast_in_dim.19
  44.1 14.7 %all_to_all.16 = bf16[4,1024,128]{1,2,0:T(8,128)(2,1)} all-to-all(bf16[4,1024,128]{1,2,0:T(8,128)(2,1)S(1)} %broadcast_in_dim.19), channel_id=1, replica_groups=mesh['z'=8,'y'=4,'x'=4,'c'=2] {'x'}, dimensions={0} | all-to-all | bytes 2097152 | tf_op jit(solution)/shard_map/all_to_all | solution.py:11
  58.9 5.3 %collective-permute-start = (bf16[4,1024,128]{1,2,0:T(8,128)(2,1)}, bf16[4,1024,128]{1,2,0:T(8,128)(2,1)}, u32[]{:S(2)}, u32[]{:S(2)}) collective-permute-start(bf16[4,1024,128]{1,2,0:T(8,128)(2,1)} %all_to_all.16), channel_id=1, source_target_pairs={{0,1},{1,0},{2,3},{3,2},{4,5},{5,4},{6,7},{7,6},{8,9},{9,8},{10,11... | collective-permute-start | bytes 3145736 | tf_op jit(solution)/shard_map/ppermute | solution.py:25
  64.1 2.6 %collective-permute-done = bf16[4,1024,128]{1,2,0:T(8,128)(2,1)} collective-permute-done((bf16[4,1024,128]{1,2,0:T(8,128)(2,1)}, bf16[4,1024,128]{1,2,0:T(8,128)(2,1)}, u32[]{:S(2)}, u32[]{:S(2)}) %collective-permute-start) | collective-permute-done | bytes 1048608 | tf_op jit(solution)/shard_map/ppermute | solution.py:25
  66.7 1.7 %select_bitcast_fusion.1 = (bf16[1,4,1024,128]{2,3,0,1:T(8,128)(2,1)S(1)}, bf16[1,4,1024,128]{2,3,0,1:T(8,128)(2,1)S(1)}) fusion(bf16[4,1024,128]{1,2,0:T(8,128)(2,1)} %all_to_all.16, bf16[4,1024,128]{1,2,0:T(8,128)(2,1)} %collective-permute-done, pred[]{:T(512)S(6)} %eq.3), kind=kLoop, calls=%fused_computation.9 | loop fusion | flops 1048576 | bytes 4194305 | tf_op jit(solution)/shard_map/stack | solution.py:27
  68.4 0.2 pad_maximum_fusion
  68.6 0.0 copy-done
  68.6 4.9 %fusion = bf16[1,1024,1536]{2,1,0:T(8,128)(2,1)} fusion(bf16[1024,1024]{0,1:T(8,128)(2,1)S(1)} %bitcast.31, bf16[1,1024,1536]{2,1,0:T(8,128)(2,1)S(1)} %copy-done), kind=kOutput, calls=%fused_computation.1 | convolution fusion | flops 3222798336 | bytes 8388608 | tf_op jit(solution)/shard_map/dot_general | solution.py:29
  (3 shorter events, 0.1 us)
Async XLA Ops:
  0.0 68.6 %copy-start = (bf16[1,1024,1536]{2,1,0:T(8,128)(2,1)S(1)}, bf16[1,1024,1536]{2,1,0:T(8,128)(2,1)}, u32[]{:S(2)}) copy-start(bf16[1,1024,1536]{2,1,0:T(8,128)(2,1)} %param.9) | copy-start | bytes 9437188
  4.5 23.2 %all-to-all-start = ((bf16[32,32,128]{2,1,0:T(8,128)(2,1)}), bf16[32,32,128]{2,1,0:T(8,128)(2,1)S(1)}, u32[]{:S(2)}, u32[]{:S(2)}) async-start(bf16[32,32,128]{2,1,0:T(8,128)(2,1)} %bitcast.32), calls=%async_computation | async-start | bytes 524288 | tf_op jit(solution)/shard_map/all_to_all | solution.py:20
  58.9 7.9 %collective-permute-start = (bf16[4,1024,128]{1,2,0:T(8,128)(2,1)}, bf16[4,1024,128]{1,2,0:T(8,128)(2,1)}, u32[]{:S(2)}, u32[]{:S(2)}) collective-permute-start(bf16[4,1024,128]{1,2,0:T(8,128)(2,1)} %all_to_all.16), channel_id=1, source_target_pairs={{0,1},{1,0},{2,3},{3,2},{4,5},{5,4},{6,7},{7,6},{8,9},{9,8},{10,11... | collective-permute-start | bytes 3145736 | tf_op jit(solution)/shard_map/ppermute | solution.py:25

commit v2 on v1

v2 whole, which is shorter than its diff:
```python
import jax
import jax.numpy as jnp
from jax import lax
from jax.experimental import pallas as pl
from jax.experimental.pallas import tpu as pltpu
from jax.sharding import Mesh, PartitionSpec as P

GRID = ("z", "y")
ROWS = 256


def project_kernel(area_ref, eofs_ref, data_ref, out_ref, scaled):
    @pl.when(pl.program_id(0) == 0)
    def _():
        for i in range(area_ref.shape[0]):
            rows = pl.ds(i * 128, 128)
            weight = jnp.transpose(jnp.broadcast_to(area_ref[i : i + 1, :], (128, 128)))
            scaled[rows, :] = (weight * eofs_ref[rows, :].astype(jnp.float32)).astype(jnp.bfloat16)

    out_ref[...] = jnp.dot(
        data_ref[...], scaled[...], preferred_element_type=jnp.float32
    ).astype(jnp.bfloat16)


def project(area, eofs, data):
    steps, points = data.shape
    modes = eofs.shape[1]
    lanes = points // 128
    return pl.pallas_call(
        project_kernel,
        grid=(steps // ROWS,),
        in_specs=[
            pl.BlockSpec((lanes, 128), lambda i: (0, 0)),
            pl.BlockSpec((points, modes), lambda i: (0, 0)),
            pl.BlockSpec((ROWS, points), lambda i: (i, 0)),
        ],
        out_specs=pl.BlockSpec((ROWS, modes), lambda i: (i, 0)),
        out_shape=jax.ShapeDtypeStruct((steps, modes), jnp.bfloat16),
        scratch_shapes=[pltpu.VMEM((points, modes), jnp.bfloat16)],
        compiler_params=pltpu.CompilerParams(vmem_limit_bytes=32 << 20),
    )(area.reshape(lanes, 128), eofs, data)


def rebuild_kernel(*refs):
    blocks, (patterns_ref, out_ref) = refs[:-2], refs[-2:]
    x, c = lax.axis_index("x"), lax.axis_index("c")
    total = None
    for i in range(4):
        source = lax.rem(x + (0, 3, 1, 2)[i], 4) * 256
        own = pl.ds(pl.multiple_of(source + c * 128, 128), 128)
        other = pl.ds(pl.multiple_of(source + (1 - c) * 128, 128), 128)
        part = jnp.dot(
            jnp.concatenate([blocks[2 * i][...], blocks[2 * i + 1][...]], axis=1),
            jnp.concatenate([patterns_ref[own, :], patterns_ref[other, :]], axis=0),
            preferred_element_type=jnp.float32,
        )
        total = part if total is None else total + part
    out_ref[...] = total.astype(jnp.bfloat16)


def rebuild(blocks, patterns):
    steps, modes = blocks[0].shape
    joined, points = patterns.shape
    return pl.pallas_call(
        rebuild_kernel,
        grid=(steps // ROWS,),
        in_specs=[pl.BlockSpec((ROWS, modes), lambda i: (i, 0))] * len(blocks)
        + [pl.BlockSpec(memory_space=pltpu.VMEM)],
        out_specs=pl.BlockSpec((ROWS, points), lambda i: (i, 0)),
        out_shape=jax.ShapeDtypeStruct((steps, points), jnp.bfloat16),
        compiler_params=pltpu.CompilerParams(vmem_limit_bytes=48 << 20),
    )(*blocks, patterns)


def shift(block, axis, by):
    count = lax.axis_size(axis)
    return lax.ppermute(block, axis, [(i, (i + by) % count) for i in range(count)])


def body(data, area, eofs, var_scale, recon_map):
    partial_comps = project(area, eofs[0], data[0])
    steps, modes = partial_comps.shape
    points = lax.axis_size("z") * lax.axis_size("y")
    pieces = partial_comps.reshape(points, steps // points, modes)
    pieces = lax.all_to_all(pieces, GRID, 0, 0, tiled=True)
    comps = jnp.sum(pieces.astype(jnp.float32), axis=0)
    own = (var_scale[0] * comps).astype(jnp.bfloat16)
    spread = jnp.broadcast_to(own[None], (points, *own.shape))
    mine = lax.all_to_all(spread, GRID, 0, 0, tiled=True).reshape(steps, modes)
    blocks = [mine, shift(mine, "x", 1), shift(mine, "x", 3), shift(mine, "x", 2)]
    blocks = [part for block in blocks for part in (block, shift(block, "c", 1))]
    return rebuild(blocks, recon_map[0])[None]


def solution(mesh):
    fine = Mesh(mesh.devices.reshape(8, 4, 4, 2), ("z", "y", "x", "c"))
    var = ("x", "c")
    placed = (
        P(var, None, GRID),
        P(GRID),
        P(var, GRID, None),
        P(var),
        P(var, None, GRID),
    )
    return jax.shard_map(
        body, mesh=fine, in_specs=placed, out_specs=P(var, None, GRID), check_vma=False
    )
```

time: 73.9 us -> 67.3 us (0.911)
  blocking collectives: 29.8 us -> 15 us
  starting transfers between devices: 17.3 us -> 28.4 us
  matrix products: 8.61 us -> 0 us
  Pallas kernels: 0 us -> 7.48 us
  other arithmetic: 1.93 us -> 0.06 us
  local copies, waits for them, and re-layouts: 2.08 us -> 3.62 us
  waiting for transfers between devices: 13.2 us -> 11.8 us
    all_to_all x2 -> x1, blocking collectives: 29.8 us -> 15 us  [body(): mine = lax.all_to_all(spread, GRID, 0, 0, tiled=True).reshape(steps, modes)]
    ppermute x1 -> x7, starting transfers between devices: 5.26 us -> 16.3 us  [shift(): lax.ppermute(block, axis, [(i, (i + by) % count) for i in range(count)])]
    dot_general x2 -> x0, matrix products: 8.61 us -> none  [the longest x1 4.94 us: body(): rebuilt = jnp.dot(joined, recon_map[0], preferred_element_type=jnp.float32)]
    pallas_call x0 -> x2, Pallas kernels: none -> 7.48 us  [the longest x1 4.88 us: rebuild(): pl.pallas_call(rebuild_kernel, grid=(steps // ROWS,), in_specs=[pl.BlockS...]
    unnamed x2 -> x8, local copies, waits for them, and re-layouts: 0.01 us -> 3.58 us
    another operation x2 -> x0, other arithmetic: 1.87 us -> none  [body(): jnp.stack([jnp.where(first, across, other), jnp.where(first, other, acros...]
    ppermute x1 -> x7, waiting for transfers between devices: 2.63 us -> 1.22 us  [shift(): lax.ppermute(block, axis, [(i, (i + by) % count) for i in range(count)])]
    broadcast_in_dim x3 -> x1, local copies, waits for them, and re-layouts: 1.24 us -> 0.04 us  [body(): spread = jnp.broadcast_to(own[None], (points, *own.shape))]
  transfers between devices with their start and end apart: 2 -> 8, of which waited for: 2 -> 3; matrix products, arithmetic and copies ran while one was open for 0% -> 0% of each run, Pallas kernels for 0% -> 0%
where the time goes in v2:
time: 67.3 us; the launch traced here: 66.9 us
  starting transfers between devices  28.4 us (42%)
  blocking collectives  15 us (22%)
  waiting for transfers between devices  11.8 us (18%)
  Pallas kernels  7.48 us (11%)
  local copies, waits for them, and re-layouts  3.62 us (5%)
  between operations  0.68 us (1%)
    ppermute x7, starting transfers between devices, shift(): lax.ppermute(block, axis, [(i, (i + by) % count) for i in range(count)])  16.3 us
    all_to_all x1, blocking collectives, body(): mine = lax.all_to_all(spread, GRID, 0, 0, tiled=True).reshape(steps, modes)  15 us
    all_to_all x1, starting transfers between devices, body(): pieces = lax.all_to_all(pieces, GRID, 0, 0, tiled=True)  12 us
    all_to_all x1, waiting for transfers between devices, body(): pieces = lax.all_to_all(pieces, GRID, 0, 0, tiled=True)  10.5 us
    pallas_call x1, Pallas kernels, rebuild(): pl.pallas_call(rebuild_kernel, grid=(steps // ROWS,), in_specs=[pl.BlockS...  4.88 us
    unnamed x8, local copies, waits for them, and re-layouts  3.58 us
    pallas_call x1, Pallas kernels, project(): pl.pallas_call(project_kernel, grid=(steps // ROWS,), in_specs=[pl.BlockS...  2.61 us
  transfers between devices with their start and end apart: 8, of which 3 were waited for; matrix products, arithmetic and copies ran while one was open for 0% of the time, Pallas kernels for 0%

profile of v2, /device:TPU:1, one launch (start us, length us, event | category | flops | bytes accessed | tf_op | source)
XLA Modules:
  0.0 66.9 jit_solution(15922477057094723762)
XLA Ops:
  0.0 0.0 copy-start
  0.0 1.9 %copy-done = bf16[1,1024,1536]{2,1,0:T(8,128)(2,1)S(1)} copy-done((bf16[1,1024,1536]{2,1,0:T(8,128)(2,1)S(1)}, bf16[1,1024,1536]{2,1,0:T(8,128)(2,1)}, u32[]{:S(2)}) %copy-start) | copy-done | bytes 3145752
  1.9 1.0 %copy-done.2 = bf16[1,1536,128]{2,1,0:T(8,128)(2,1)S(1)} copy-done((bf16[1,1536,128]{2,1,0:T(8,128)(2,1)S(1)}, bf16[1,1536,128]{2,1,0:T(8,128)(2,1)}, u32[]{:S(2)}) %copy-start.2) | copy-done | bytes 393240
  2.9 0.7 %copy-done.3 = f32[1536]{0:T(1024)S(1)} copy-done((f32[1536]{0:T(1024)S(1)}, f32[1536]{0:T(1024)}, u32[]{:S(2)}) %copy-start.3) | copy-done | bytes 6168
  3.6 2.6 %shard_map.55 = bf16[1024,128]{1,0:T(8,128)(2,1)} custom-call(f32[12,128]{1,0:T(8,128)S(1)} %bitcast.17, bf16[1536,128]{1,0:T(8,128)(2,1)S(1)} %bitcast.16, bf16[1024,1536]{1,0:T(8,128)(2,1)S(1)} %bitcast.9), custom_call_target="tpu_custom_call" | custom-call | tf_op jit(solution)/shard_map/pallas_call | solution.py:29
  6.2 12.0 %all-to-all-start = ((bf16[32,32,128]{2,1,0:T(8,128)(2,1)}), bf16[32,32,128]{2,1,0:T(8,128)(2,1)S(1)}, u32[]{:S(2)}, u32[]{:S(2)}) async-start(bf16[32,32,128]{2,1,0:T(8,128)(2,1)} %bitcast.4), calls=%async_computation | async-start | bytes 524288 | tf_op jit(solution)/shard_map/all_to_all | solution.py:85
  18.9 10.5 %all-to-all-done = bf16[32,32,128]{2,1,0:T(8,128)(2,1)S(1)} async-done(((bf16[32,32,128]{2,1,0:T(8,128)(2,1)}), bf16[32,32,128]{2,1,0:T(8,128)(2,1)S(1)}, u32[]{:S(2)}, u32[]{:S(2)}) %all-to-all-start) | async-done | bytes 262176 | tf_op jit(solution)/shard_map/all_to_all | solution.py:85
  29.5 15.0 %all_to_all.10 = bf16[32,32,128]{2,1,0:T(8,128)(2,1)S(1)} all-to-all(bf16[32,32,128]{2,1,0:T(8,128)(2,1)S(1)} %broadcast_in_dim.4), channel_id=1, replica_groups=mesh['z'=8,'y'=4,'x'=4,'c'=2] {'z','y'}, dimensions={0} | all-to-all | bytes 524288 | tf_op jit(solution)/shard_map/all_to_all | solution.py:89
  44.5 2.7 %collective-permute-start.5 = (bf16[1024,128]{1,0:T(8,128)(2,1)S(1)}, bf16[1024,128]{1,0:T(8,128)(2,1)S(1)}, u32[]{:S(2)}, u32[]{:S(2)}) collective-permute-start(bf16[1024,128]{1,0:T(8,128)(2,1)S(1)} %bitcast.11), channel_id=1, source_target_pairs={{0,4},{2,6},{4,0},{6,2},{1,5},{3,7},{5,1},{7,3},{8,12},{10,14},{12... | collective-permute-start | bytes 786440 | tf_op jit(solution)/shard_map/ppermute | solution.py:77
  47.2 0.9 %collective-permute-start.3 = (bf16[1024,128]{1,0:T(8,128)(2,1)S(1)}, bf16[1024,128]{1,0:T(8,128)(2,1)S(1)}, u32[]{:S(2)}, u32[]{:S(2)}) collective-permute-start(bf16[1024,128]{1,0:T(8,128)(2,1)S(1)} %bitcast.12), channel_id=1, source_target_pairs={{0,6},{2,0},{4,2},{6,4},{1,7},{3,1},{5,3},{7,5},{8,14},{10,8},{12,... | collective-permute-start | bytes 786440 | tf_op jit(solution)/shard_map/ppermute | solution.py:77
  48.1 0.6 collective-permute-start.1
  48.7 4.6 %collective-permute-start = (bf16[1024,128]{1,0:T(8,128)(2,1)S(1)}, bf16[1024,128]{1,0:T(8,128)(2,1)S(1)}, u32[]{:S(2)}, u32[]{:S(2)}) collective-permute-start(bf16[1024,128]{1,0:T(8,128)(2,1)S(1)} %bitcast.14), channel_id=1, source_target_pairs={{0,1},{1,0},{2,3},{3,2},{4,5},{5,4},{6,7},{7,6},{8,9},{9,8},{10,11... | collective-permute-start | bytes 786440 | tf_op jit(solution)/shard_map/ppermute | solution.py:77
  53.3 0.0 collective-permute-done.5.refs_6_
  53.3 4.3 %collective-permute-start.6 = (bf16[1024,128]{1,0:T(8,128)(2,1)S(1)}, bf16[1024,128]{1,0:T(8,128)(2,1)S(1)}, u32[]{:S(2)}, u32[]{:S(2)}) collective-permute-start(bf16[1024,128]{1,0:T(8,128)(2,1)S(1)} %collective-permute-done.5.refs_6_), channel_id=1, source_target_pairs={{0,1},{1,0},{2,3},{3,2},{4,5},{5,4},{6,7},{7,6},{8,9},{9,8},{10,11... | collective-permute-start | bytes 786440 | tf_op jit(solution)/shard_map/ppermute | solution.py:77
  57.6 0.0 collective-permute-done.3.refs_4_
  57.6 2.9 %collective-permute-start.4 = (bf16[1024,128]{1,0:T(8,128)(2,1)S(1)}, bf16[1024,128]{1,0:T(8,128)(2,1)S(1)}, u32[]{:S(2)}, u32[]{:S(2)}) collective-permute-start(bf16[1024,128]{1,0:T(8,128)(2,1)S(1)} %collective-permute-done.3.refs_4_), channel_id=1, source_target_pairs={{0,1},{1,0},{2,3},{3,2},{4,5},{5,4},{6,7},{7,6},{8,9},{9,8},{10,11... | collective-permute-start | bytes 786440 | tf_op jit(solution)/shard_map/ppermute | solution.py:77
  60.5 0.0 collective-permute-done.1.refs_2_
  60.5 0.3 collective-permute-start.2
  60.8 0.0 collective-permute-done.refs_1_
  60.9 0.0 collective-permute-done.6.refs_7_
  60.9 0.8 %collective-permute-done.4.refs_5_ = bf16[1024,128]{1,0:T(8,128)(2,1)S(1)} collective-permute-done((bf16[1024,128]{1,0:T(8,128)(2,1)S(1)}, bf16[1024,128]{1,0:T(8,128)(2,1)S(1)}, u32[]{:S(2)}, u32[]{:S(2)}) %collective-permute-start.4) | collective-permute-done | bytes 262176 | tf_op jit(solution)/shard_map/ppermute | solution.py:77
  61.7 0.4 collective-permute-done.2.refs_3_
  62.1 0.0 copy-done.1
  62.1 4.9 %shard_map.56 = bf16[1024,1536]{1,0:T(8,128)(2,1)} custom-call(bf16[1024,128]{1,0:T(8,128)(2,1)S(1)} %bitcast.15, bf16[1024,128]{1,0:T(8,128)(2,1)S(1)} %collective-permute-done.refs_1_, bf16[1024,128]{1,0:T(8,128)(2,1)S(1)} %collective-permute-done.1.refs_2_, bf16[1024,128]{1,0:T(8,128)(2,1)S(1)} %collective-permute-done.2.refs_3_, ...), custom_call_target="tpu_custom_call" | custom-call | tf_op jit(solution)/shard_map/pallas_call | solution.py:64
  (6 shorter events, 0.1 us)
Async XLA Ops:
  0.0 1.9 %copy-start = (bf16[1,1024,1536]{2,1,0:T(8,128)(2,1)S(1)}, bf16[1,1024,1536]{2,1,0:T(8,128)(2,1)}, u32[]{:S(2)}) copy-start(bf16[1,1024,1536]{2,1,0:T(8,128)(2,1)} %param.5) | copy-start | bytes 9437188
  1.9 1.0 %copy-start.2 = (bf16[1,1536,128]{2,1,0:T(8,128)(2,1)S(1)}, bf16[1,1536,128]{2,1,0:T(8,128)(2,1)}, u32[]{:S(2)}) copy-start(bf16[1,1536,128]{2,1,0:T(8,128)(2,1)} %param.7) | copy-start | bytes 1179652
  2.9 0.7 %copy-start.3 = (f32[1536]{0:T(1024)S(1)}, f32[1536]{0:T(1024)}, u32[]{:S(2)}) copy-start(f32[1536]{0:T(1024)} %param.6) | copy-start | bytes 18436
  3.6 58.5 %copy-start.1 = (bf16[1,1024,1536]{2,1,0:T(8,128)(2,1)S(1)}, bf16[1,1024,1536]{2,1,0:T(8,128)(2,1)}, u32[]{:S(2)}) copy-start(bf16[1,1024,1536]{2,1,0:T(8,128)(2,1)} %param.9) | copy-start | bytes 9437188
  6.2 23.2 %all-to-all-start = ((bf16[32,32,128]{2,1,0:T(8,128)(2,1)}), bf16[32,32,128]{2,1,0:T(8,128)(2,1)S(1)}, u32[]{:S(2)}, u32[]{:S(2)}) async-start(bf16[32,32,128]{2,1,0:T(8,128)(2,1)} %bitcast.4), calls=%async_computation | async-start | bytes 524288 | tf_op jit(solution)/shard_map/all_to_all | solution.py:85
  44.5 8.8 %collective-permute-start.5 = (bf16[1024,128]{1,0:T(8,128)(2,1)S(1)}, bf16[1024,128]{1,0:T(8,128)(2,1)S(1)}, u32[]{:S(2)}, u32[]{:S(2)}) collective-permute-start(bf16[1024,128]{1,0:T(8,128)(2,1)S(1)} %bitcast.11), channel_id=1, source_target_pairs={{0,4},{2,6},{4,0},{6,2},{1,5},{3,7},{5,1},{7,3},{8,12},{10,14},{12... | collective-permute-start | bytes 786440 | tf_op jit(solution)/shard_map/ppermute | solution.py:77
  47.2 10.4 %collective-permute-start.3 = (bf16[1024,128]{1,0:T(8,128)(2,1)S(1)}, bf16[1024,128]{1,0:T(8,128)(2,1)S(1)}, u32[]{:S(2)}, u32[]{:S(2)}) collective-permute-start(bf16[1024,128]{1,0:T(8,128)(2,1)S(1)} %bitcast.12), channel_id=1, source_target_pairs={{0,6},{2,0},{4,2},{6,4},{1,7},{3,1},{5,3},{7,5},{8,14},{10,8},{12,... | collective-permute-start | bytes 786440 | tf_op jit(solution)/shard_map/ppermute | solution.py:77
  48.1 12.4 %collective-permute-start.1 = (bf16[1024,128]{1,0:T(8,128)(2,1)S(1)}, bf16[1024,128]{1,0:T(8,128)(2,1)S(1)}, u32[]{:S(2)}, u32[]{:S(2)}) collective-permute-start(bf16[1024,128]{1,0:T(8,128)(2,1)S(1)} %bitcast.13), channel_id=1, source_target_pairs={{0,2},{2,4},{4,6},{6,0},{1,3},{3,5},{5,7},{7,1},{8,10},{10,12},{12... | collective-permute-start | bytes 786440 | tf_op jit(solution)/shard_map/ppermute | solution.py:77
  48.7 12.1 %collective-permute-start = (bf16[1024,128]{1,0:T(8,128)(2,1)S(1)}, bf16[1024,128]{1,0:T(8,128)(2,1)S(1)}, u32[]{:S(2)}, u32[]{:S(2)}) collective-permute-start(bf16[1024,128]{1,0:T(8,128)(2,1)S(1)} %bitcast.14), channel_id=1, source_target_pairs={{0,1},{1,0},{2,3},{3,2},{4,5},{5,4},{6,7},{7,6},{8,9},{9,8},{10,11... | collective-permute-start | bytes 786440 | tf_op jit(solution)/shard_map/ppermute | solution.py:77
  53.3 7.5 %collective-permute-start.6 = (bf16[1024,128]{1,0:T(8,128)(2,1)S(1)}, bf16[1024,128]{1,0:T(8,128)(2,1)S(1)}, u32[]{:S(2)}, u32[]{:S(2)}) collective-permute-start(bf16[1024,128]{1,0:T(8,128)(2,1)S(1)} %collective-permute-done.5.refs_6_), channel_id=1, source_target_pairs={{0,1},{1,0},{2,3},{3,2},{4,5},{5,4},{6,7},{7,6},{8,9},{9,8},{10,11... | collective-permute-start | bytes 786440 | tf_op jit(solution)/shard_map/ppermute | solution.py:77
  57.6 4.0 %collective-permute-start.4 = (bf16[1024,128]{1,0:T(8,128)(2,1)S(1)}, bf16[1024,128]{1,0:T(8,128)(2,1)S(1)}, u32[]{:S(2)}, u32[]{:S(2)}) collective-permute-start(bf16[1024,128]{1,0:T(8,128)(2,1)S(1)} %collective-permute-done.3.refs_4_), channel_id=1, source_target_pairs={{0,1},{1,0},{2,3},{3,2},{4,5},{5,4},{6,7},{7,6},{8,9},{9,8},{10,11... | collective-permute-start | bytes 786440 | tf_op jit(solution)/shard_map/ppermute | solution.py:77
  60.5 1.5 %collective-permute-start.2 = (bf16[1024,128]{1,0:T(8,128)(2,1)S(1)}, bf16[1024,128]{1,0:T(8,128)(2,1)S(1)}, u32[]{:S(2)}, u32[]{:S(2)}) collective-permute-start(bf16[1024,128]{1,0:T(8,128)(2,1)S(1)} %collective-permute-done.1.refs_2_), channel_id=1, source_target_pairs={{0,1},{1,0},{2,3},{3,2},{4,5},{5,4},{6,7},{7,6},{8,9},{9,8},{10,11... | collective-permute-start | bytes 786440 | tf_op jit(solution)/shard_map/ppermute | solution.py:77

commit v3 on v1

v3 whole, which is shorter than its diff:
```python
import functools

import jax
import jax.numpy as jnp
from jax import lax
from jax.experimental import pallas as pl
from jax.experimental.pallas import tpu as pltpu
from jax.sharding import Mesh, PartitionSpec as P

GRID = ("z", "y")
ROWS = 256
COLUMNS = 512


def project_kernel(area_hbm, eofs_hbm, data_hbm, out_ref, area, eofs, scaled, data, sems):
    pieces = data_hbm.shape[0] // ROWS
    weights = pltpu.make_async_copy(area_hbm, area, sems.at[pieces + 1])
    weights.start()
    loads = [pltpu.make_async_copy(eofs_hbm, eofs, sems.at[pieces])]
    for i in range(pieces):
        rows = pl.ds(i * ROWS, ROWS)
        loads.append(pltpu.make_async_copy(data_hbm.at[rows, :], data.at[rows, :], sems.at[i]))
    for load in loads:
        load.start()
    weights.wait()
    loads[0].wait()
    for i in range(area.shape[0]):
        rows = pl.ds(i * 128, 128)
        weight = jnp.transpose(jnp.broadcast_to(area[i : i + 1, :], (128, 128)))
        scaled[rows, :] = (weight * eofs[rows, :].astype(jnp.float32)).astype(jnp.bfloat16)
    for i in range(pieces):
        rows = pl.ds(i * ROWS, ROWS)
        loads[1 + i].wait()
        out_ref[rows, :] = jnp.dot(
            data[rows, :], scaled[...], preferred_element_type=jnp.float32
        ).astype(jnp.bfloat16)


def project(area, eofs, data):
    steps, points = data.shape
    modes = eofs.shape[1]
    lanes = points // 128
    return pl.pallas_call(
        project_kernel,
        in_specs=[
            pl.BlockSpec(memory_space=pltpu.HBM),
            pl.BlockSpec(memory_space=pltpu.HBM),
            pl.BlockSpec(memory_space=pltpu.HBM),
        ],
        out_specs=pl.BlockSpec(memory_space=pltpu.VMEM),
        out_shape=pltpu.VMEM((steps, modes), jnp.bfloat16),
        scratch_shapes=[
            pltpu.VMEM((lanes, 128), jnp.float32),
            pltpu.VMEM((points, modes), jnp.bfloat16),
            pltpu.VMEM((points, modes), jnp.bfloat16),
            pltpu.VMEM((steps, points), jnp.bfloat16),
            pltpu.SemaphoreType.DMA((steps // ROWS + 2,)),
        ],
        compiler_params=pltpu.CompilerParams(vmem_limit_bytes=32 << 20),
    )(
        pltpu.with_memory_space_constraint(area.reshape(lanes, 128), pltpu.HBM),
        pltpu.with_memory_space_constraint(eofs, pltpu.HBM),
        pltpu.with_memory_space_constraint(data, pltpu.HBM),
    )


VMEM = pl.BlockSpec(memory_space=pltpu.VMEM)


def operands(blocks, sources, patterns_ref):
    x, c = lax.axis_index("x"), lax.axis_index("c")
    owners = []
    for source in sources:
        base = lax.rem(x + source, 4) * 256
        owners += [base + c * 128, base + (1 - c) * 128]
    owners = [pl.ds(pl.multiple_of(owner, 128), 128) for owner in owners]

    def joined(rows):
        return jnp.concatenate([block[rows, :] for block in blocks], axis=1)

    def patterns(columns):
        return jnp.concatenate([patterns_ref[k, columns] for k in owners], axis=0)

    return joined, patterns


def start_kernel(sources, *refs):
    blocks, patterns_ref, total_ref = refs[:-2], refs[-2], refs[-1]
    steps, points = total_ref.shape
    joined, patterns = operands(blocks, sources, patterns_ref)
    for i in range(steps // ROWS):
        rows = pl.ds(i * ROWS, ROWS)
        for j in range(points // COLUMNS):
            columns = pl.ds(j * COLUMNS, COLUMNS)
            total_ref[rows, columns] = jnp.dot(
                joined(rows), patterns(columns), preferred_element_type=jnp.float32
            )


def finish_kernel(sources, *refs):
    blocks, (patterns_ref, total_ref, out_hbm, out, sems) = refs[:-5], refs[-5:]
    steps, points = total_ref.shape
    joined, patterns = operands(blocks, sources, patterns_ref)
    stores = []
    for i in range(steps // 128):
        rows = pl.ds(i * 128, 128)
        for j in range(points // COLUMNS):
            columns = pl.ds(j * COLUMNS, COLUMNS)
            part = jnp.dot(joined(rows), patterns(columns), preferred_element_type=jnp.float32)
            out[rows, columns] = (total_ref[rows, columns] + part).astype(jnp.bfloat16)
        stores.append(pltpu.make_async_copy(out.at[rows, :], out_hbm.at[rows, :], sems.at[i]))
        stores[-1].start()
    for store in stores:
        store.wait()


def start(blocks, sources, patterns):
    steps, points = blocks[0].shape[0], patterns.shape[1]
    return pl.pallas_call(
        functools.partial(start_kernel, sources),
        in_specs=[VMEM] * (len(blocks) + 1),
        out_specs=VMEM,
        out_shape=pltpu.VMEM((steps, points), jnp.float32),
        compiler_params=pltpu.CompilerParams(vmem_limit_bytes=16 << 20),
    )(*blocks, patterns)


def finish(blocks, sources, patterns, total):
    steps, points = total.shape
    return pl.pallas_call(
        functools.partial(finish_kernel, sources),
        in_specs=[VMEM] * (len(blocks) + 2),
        out_specs=pl.BlockSpec(memory_space=pltpu.HBM),
        out_shape=jax.ShapeDtypeStruct((steps, points), jnp.bfloat16),
        scratch_shapes=[
            pltpu.VMEM((steps, points), jnp.bfloat16),
            pltpu.SemaphoreType.DMA((steps // 128,)),
        ],
        compiler_params=pltpu.CompilerParams(vmem_limit_bytes=16 << 20),
    )(*blocks, patterns, total)


def shift(block, axis, by):
    count = lax.axis_size(axis)
    return lax.ppermute(block, axis, [(i, (i + by) % count) for i in range(count)])


def exchange_and_rebuild(mine, patterns):
    blocks = [mine, shift(mine, "x", 2), shift(mine, "x", 1), shift(mine, "x", 3)]
    blocks = [(block, shift(block, "c", 1)) for block in blocks]
    early = [part for pair in blocks[:2] for part in pair]
    late = [part for pair in blocks[2:] for part in pair]
    total = start(early, (0, 2), patterns)
    return finish(late, (3, 1), patterns, total)


def body(data, area, eofs, var_scale, recon_map):
    partial_comps = project(area, eofs[0], data[0])
    patterns, partial_comps = lax.optimization_barrier((recon_map[0], partial_comps))
    steps, modes = partial_comps.shape
    points = lax.axis_size("z") * lax.axis_size("y")
    pieces = partial_comps.reshape(points, steps // points, modes)
    pieces = lax.all_to_all(pieces, GRID, 0, 0, tiled=True)
    comps = jnp.sum(pieces.astype(jnp.float32), axis=0)
    own = (var_scale[0] * comps).astype(jnp.bfloat16)
    spread = jnp.broadcast_to(own[None], (points, *own.shape))
    mine = lax.all_to_all(spread, GRID, 0, 0, tiled=True).reshape(steps, modes)
    return exchange_and_rebuild(mine, patterns)[None]


def solution(mesh):
    fine = Mesh(mesh.devices.reshape(8, 4, 4, 2), ("z", "y", "x", "c"))
    var = ("x", "c")
    placed = (
        P(var, None, GRID),
        P(GRID),
        P(var, GRID, None),
        P(var),
        P(var, None, GRID),
    )
    return jax.shard_map(
        body, mesh=fine, in_specs=placed, out_specs=P(var, None, GRID), check_vma=False
    )
```

time: 73.9 us -> 63 us (0.85)
  blocking collectives: 29.8 us -> 15 us
  starting transfers between devices: 17.3 us -> 28.4 us
  matrix products: 8.61 us -> 0 us
  Pallas kernels: 0 us -> 8.07 us
  waiting for transfers between devices: 13.2 us -> 10.6 us
  local copies, waits for them, and re-layouts: 2.08 us -> 0.04 us
  other arithmetic: 1.93 us -> 0.06 us
    all_to_all x2 -> x1, blocking collectives: 29.8 us -> 15 us  [body(): mine = lax.all_to_all(spread, GRID, 0, 0, tiled=True).reshape(steps, modes)]
    ppermute x1 -> x7, starting transfers between devices: 5.26 us -> 16.3 us  [shift(): lax.ppermute(block, axis, [(i, (i + by) % count) for i in range(count)])]
    dot_general x2 -> x0, matrix products: 8.61 us -> none  [the longest x1 4.94 us: body(): rebuilt = jnp.dot(joined, recon_map[0], preferred_element_type=jnp.float32)]
    pallas_call x0 -> x3, Pallas kernels: none -> 8.07 us  [the longest x1 3.62 us: project(): pl.pallas_call(project_kernel, in_specs=[pl.BlockSpec(memory_space=pltpu....]
    ppermute x1 -> x7, waiting for transfers between devices: 2.63 us -> 0.02 us  [shift(): lax.ppermute(block, axis, [(i, (i + by) % count) for i in range(count)])]
    another operation x2 -> x0, other arithmetic: 1.87 us -> none  [body(): jnp.stack([jnp.where(first, across, other), jnp.where(first, other, acros...]
    broadcast_in_dim x3 -> x1, local copies, waits for them, and re-layouts: 1.24 us -> 0.04 us  [body(): spread = jnp.broadcast_to(own[None], (points, *own.shape))]
    convert_element_type x1 -> x0, local copies, waits for them, and re-layouts: 0.84 us -> none  [body(): partial_comps.astype(jnp.bfloat16).reshape(points, steps // points, modes)]
  transfers between devices with their start and end apart: 2 -> 8, of which waited for: 2 -> 1; matrix products, arithmetic and copies ran while one was open for 0% -> 0% of each run, Pallas kernels for 0% -> 3%
where the time goes in v3:
time: 63 us; the launch traced here: 62.8 us
  starting transfers between devices  28.4 us (45%)
  blocking collectives  15 us (24%)
  waiting for transfers between devices  10.6 us (17%)
  Pallas kernels  8.07 us (13%)
  between operations  0.71 us (1%)
    ppermute x7, starting transfers between devices, shift(): lax.ppermute(block, axis, [(i, (i + by) % count) for i in range(count)])  16.3 us
    all_to_all x1, blocking collectives, body(): mine = lax.all_to_all(spread, GRID, 0, 0, tiled=True).reshape(steps, modes)  15 us
    all_to_all x1, starting transfers between devices, body(): pieces = lax.all_to_all(pieces, GRID, 0, 0, tiled=True)  12 us
    all_to_all x1, waiting for transfers between devices, body(): pieces = lax.all_to_all(pieces, GRID, 0, 0, tiled=True)  10.5 us
    pallas_call x1, Pallas kernels, project(): pl.pallas_call(project_kernel, in_specs=[pl.BlockSpec(memory_space=pltpu....  3.62 us
    pallas_call x1, Pallas kernels, finish(): pl.pallas_call(functools.partial(finish_kernel, sources), in_specs=[VMEM]...  2.65 us
    pallas_call x1, Pallas kernels, start(): pl.pallas_call(functools.partial(start_kernel, sources), in_specs=[VMEM]...  1.81 us
  transfers between devices with their start and end apart: 8, of which 1 were waited for; matrix products, arithmetic and copies ran while one was open for 0% of the time, Pallas kernels for 3%

profile of v3, /device:TPU:1, one launch (start us, length us, event | category | flops | bytes accessed | tf_op | source)
XLA Modules:
  0.0 62.8 jit_solution(944993802579958633)
XLA Ops:
  0.0 0.0 copy-start
  0.0 3.6 %shard_map.55 = bf16[1024,128]{1,0:T(8,128)(2,1)} custom-call(f32[12,128]{1,0:T(8,128)} %bitcast.18, bf16[1536,128]{1,0:T(8,128)(2,1)} %bitcast.17, bf16[1024,1536]{1,0:T(8,128)(2,1)} %bitcast.16), custom_call_target="tpu_custom_call" | custom-call | tf_op jit(solution)/shard_map/pallas_call | solution.py:43
  3.6 12.0 %all-to-all-start = ((bf16[32,32,128]{2,1,0:T(8,128)(2,1)}), bf16[32,32,128]{2,1,0:T(8,128)(2,1)S(1)}, u32[]{:S(2)}, u32[]{:S(2)}) async-start(bf16[32,32,128]{2,1,0:T(8,128)(2,1)} %bitcast.5), calls=%async_computation | async-start | bytes 524288 | tf_op jit(solution)/shard_map/all_to_all | solution.py:163
  16.3 10.5 %all-to-all-done = bf16[32,32,128]{2,1,0:T(8,128)(2,1)S(1)} async-done(((bf16[32,32,128]{2,1,0:T(8,128)(2,1)}), bf16[32,32,128]{2,1,0:T(8,128)(2,1)S(1)}, u32[]{:S(2)}, u32[]{:S(2)}) %all-to-all-start) | async-done | bytes 262176 | tf_op jit(solution)/shard_map/all_to_all | solution.py:163
  27.0 15.0 %all_to_all.10 = bf16[32,32,128]{2,1,0:T(8,128)(2,1)S(1)} all-to-all(bf16[32,32,128]{2,1,0:T(8,128)(2,1)S(1)} %broadcast_in_dim.4), channel_id=1, replica_groups=mesh['z'=8,'y'=4,'x'=4,'c'=2] {'z','y'}, dimensions={0} | all-to-all | bytes 524288 | tf_op jit(solution)/shard_map/all_to_all | solution.py:167
  41.9 2.7 %collective-permute-start.5 = (bf16[1024,128]{1,0:T(8,128)(2,1)S(1)}, bf16[1024,128]{1,0:T(8,128)(2,1)S(1)}, u32[]{:S(2)}, u32[]{:S(2)}) collective-permute-start(bf16[1024,128]{1,0:T(8,128)(2,1)S(1)} %bitcast.11), channel_id=1, source_target_pairs={{0,4},{2,6},{4,0},{6,2},{1,5},{3,7},{5,1},{7,3},{8,12},{10,14},{12... | collective-permute-start | bytes 786440 | tf_op jit(solution)/shard_map/ppermute | solution.py:145
  44.7 0.9 %collective-permute-start.2 = (bf16[1024,128]{1,0:T(8,128)(2,1)S(1)}, bf16[1024,128]{1,0:T(8,128)(2,1)S(1)}, u32[]{:S(2)}, u32[]{:S(2)}) collective-permute-start(bf16[1024,128]{1,0:T(8,128)(2,1)S(1)} %bitcast.12), channel_id=1, source_target_pairs={{0,6},{2,0},{4,2},{6,4},{1,7},{3,1},{5,3},{7,5},{8,14},{10,8},{12,... | collective-permute-start | bytes 786440 | tf_op jit(solution)/shard_map/ppermute | solution.py:145
  45.5 0.6 collective-permute-start
  46.2 4.6 %collective-permute-start.4 = (bf16[1024,128]{1,0:T(8,128)(2,1)S(1)}, bf16[1024,128]{1,0:T(8,128)(2,1)S(1)}, u32[]{:S(2)}, u32[]{:S(2)}) collective-permute-start(bf16[1024,128]{1,0:T(8,128)(2,1)S(1)} %bitcast.14), channel_id=1, source_target_pairs={{0,1},{1,0},{2,3},{3,2},{4,5},{5,4},{6,7},{7,6},{8,9},{9,8},{10,11... | collective-permute-start | bytes 786440 | tf_op jit(solution)/shard_map/ppermute | solution.py:145
  50.8 0.0 collective-permute-done.5.refs_2_
  50.8 4.3 %collective-permute-start.6 = (bf16[1024,128]{1,0:T(8,128)(2,1)S(1)}, bf16[1024,128]{1,0:T(8,128)(2,1)S(1)}, u32[]{:S(2)}, u32[]{:S(2)}) collective-permute-start(bf16[1024,128]{1,0:T(8,128)(2,1)S(1)} %collective-permute-done.5.refs_2_), channel_id=1, source_target_pairs={{0,1},{1,0},{2,3},{3,2},{4,5},{5,4},{6,7},{7,6},{8,9},{9,8},{10,11... | collective-permute-start | bytes 786440 | tf_op jit(solution)/shard_map/ppermute | solution.py:145
  55.1 0.0 collective-permute-done.2.refs_2_
  55.1 2.9 %collective-permute-start.3 = (bf16[1024,128]{1,0:T(8,128)(2,1)S(1)}, bf16[1024,128]{1,0:T(8,128)(2,1)S(1)}, u32[]{:S(2)}, u32[]{:S(2)}) collective-permute-start(bf16[1024,128]{1,0:T(8,128)(2,1)S(1)} %collective-permute-done.2.refs_2_), channel_id=1, source_target_pairs={{0,1},{1,0},{2,3},{3,2},{4,5},{5,4},{6,7},{7,6},{8,9},{9,8},{10,11... | collective-permute-start | bytes 786440 | tf_op jit(solution)/shard_map/ppermute | solution.py:145
  58.0 0.0 collective-permute-done.refs_0_
  58.0 0.3 collective-permute-start.1
  58.3 0.0 collective-permute-done.4.refs_1_
  58.3 0.0 collective-permute-done.6.refs_3_
  58.3 0.0 copy-done
  58.3 1.8 %shard_map.56.refs_5_ = f32[1024,1536]{1,0:T(8,128)S(1)} custom-call(bf16[1024,128]{1,0:T(8,128)(2,1)S(1)} %bitcast.15, bf16[1024,128]{1,0:T(8,128)(2,1)S(1)} %collective-permute-done.4.refs_1_, bf16[1024,128]{1,0:T(8,128)(2,1)S(1)} %collective-permute-done.5.refs_2_, bf16[1024,128]{1,0:T(8,128)(2,1)S(1)} %collective-permute-done.6.refs_3_, ...), custom_call_target="tpu_custom_call" | custom-call | tf_op jit(solution)/shard_map/pallas_call | solution.py:119
  60.1 0.0 collective-permute-done.3.refs_3_
  60.1 0.0 collective-permute-done.1.refs_1_
  60.1 2.6 %shard_map.57 = bf16[1024,1536]{1,0:T(8,128)(2,1)} custom-call(bf16[1024,128]{1,0:T(8,128)(2,1)S(1)} %collective-permute-done.refs_0_, bf16[1024,128]{1,0:T(8,128)(2,1)S(1)} %collective-permute-done.1.refs_1_, bf16[1024,128]{1,0:T(8,128)(2,1)S(1)} %collective-permute-done.2.refs_2_, bf16[1024,128]{1,0:T(8,128)(2,1)S(1)} %collective-permute-done.3.refs_3_, ...), custom_call_target="tpu_custom_call" | custom-call | tf_op jit(solution)/shard_map/pallas_call | solution.py:130
  (3 shorter events, 0.1 us)
Async XLA Ops:
  0.0 58.3 %copy-start = (bf16[1,1024,1536]{2,1,0:T(8,128)(2,1)S(1)}, bf16[1,1024,1536]{2,1,0:T(8,128)(2,1)}, u32[]{:S(2)}) copy-start(bf16[1,1024,1536]{2,1,0:T(8,128)(2,1)} %param.9) | copy-start | bytes 9437188
  3.6 23.2 %all-to-all-start = ((bf16[32,32,128]{2,1,0:T(8,128)(2,1)}), bf16[32,32,128]{2,1,0:T(8,128)(2,1)S(1)}, u32[]{:S(2)}, u32[]{:S(2)}) async-start(bf16[32,32,128]{2,1,0:T(8,128)(2,1)} %bitcast.5), calls=%async_computation | async-start | bytes 524288 | tf_op jit(solution)/shard_map/all_to_all | solution.py:163
  41.9 8.8 %collective-permute-start.5 = (bf16[1024,128]{1,0:T(8,128)(2,1)S(1)}, bf16[1024,128]{1,0:T(8,128)(2,1)S(1)}, u32[]{:S(2)}, u32[]{:S(2)}) collective-permute-start(bf16[1024,128]{1,0:T(8,128)(2,1)S(1)} %bitcast.11), channel_id=1, source_target_pairs={{0,4},{2,6},{4,0},{6,2},{1,5},{3,7},{5,1},{7,3},{8,12},{10,14},{12... | collective-permute-start | bytes 786440 | tf_op jit(solution)/shard_map/ppermute | solution.py:145
  44.7 10.4 %collective-permute-start.2 = (bf16[1024,128]{1,0:T(8,128)(2,1)S(1)}, bf16[1024,128]{1,0:T(8,128)(2,1)S(1)}, u32[]{:S(2)}, u32[]{:S(2)}) collective-permute-start(bf16[1024,128]{1,0:T(8,128)(2,1)S(1)} %bitcast.12), channel_id=1, source_target_pairs={{0,6},{2,0},{4,2},{6,4},{1,7},{3,1},{5,3},{7,5},{8,14},{10,8},{12,... | collective-permute-start | bytes 786440 | tf_op jit(solution)/shard_map/ppermute | solution.py:145
  45.5 12.4 %collective-permute-start = (bf16[1024,128]{1,0:T(8,128)(2,1)S(1)}, bf16[1024,128]{1,0:T(8,128)(2,1)S(1)}, u32[]{:S(2)}, u32[]{:S(2)}) collective-permute-start(bf16[1024,128]{1,0:T(8,128)(2,1)S(1)} %bitcast.13), channel_id=1, source_target_pairs={{0,2},{2,4},{4,6},{6,0},{1,3},{3,5},{5,7},{7,1},{8,10},{10,12},{12... | collective-permute-start | bytes 786440 | tf_op jit(solution)/shard_map/ppermute | solution.py:145
  46.2 12.1 %collective-permute-start.4 = (bf16[1024,128]{1,0:T(8,128)(2,1)S(1)}, bf16[1024,128]{1,0:T(8,128)(2,1)S(1)}, u32[]{:S(2)}, u32[]{:S(2)}) collective-permute-start(bf16[1024,128]{1,0:T(8,128)(2,1)S(1)} %bitcast.14), channel_id=1, source_target_pairs={{0,1},{1,0},{2,3},{3,2},{4,5},{5,4},{6,7},{7,6},{8,9},{9,8},{10,11... | collective-permute-start | bytes 786440 | tf_op jit(solution)/shard_map/ppermute | solution.py:145
  50.8 7.5 %collective-permute-start.6 = (bf16[1024,128]{1,0:T(8,128)(2,1)S(1)}, bf16[1024,128]{1,0:T(8,128)(2,1)S(1)}, u32[]{:S(2)}, u32[]{:S(2)}) collective-permute-start(bf16[1024,128]{1,0:T(8,128)(2,1)S(1)} %collective-permute-done.5.refs_2_), channel_id=1, source_target_pairs={{0,1},{1,0},{2,3},{3,2},{4,5},{5,4},{6,7},{7,6},{8,9},{9,8},{10,11... | collective-permute-start | bytes 786440 | tf_op jit(solution)/shard_map/ppermute | solution.py:145
  55.1 5.0 %collective-permute-start.3 = (bf16[1024,128]{1,0:T(8,128)(2,1)S(1)}, bf16[1024,128]{1,0:T(8,128)(2,1)S(1)}, u32[]{:S(2)}, u32[]{:S(2)}) collective-permute-start(bf16[1024,128]{1,0:T(8,128)(2,1)S(1)} %collective-permute-done.2.refs_2_), channel_id=1, source_target_pairs={{0,1},{1,0},{2,3},{3,2},{4,5},{5,4},{6,7},{7,6},{8,9},{9,8},{10,11... | collective-permute-start | bytes 786440 | tf_op jit(solution)/shard_map/ppermute | solution.py:145
  58.0 2.2 %collective-permute-start.1 = (bf16[1024,128]{1,0:T(8,128)(2,1)S(1)}, bf16[1024,128]{1,0:T(8,128)(2,1)S(1)}, u32[]{:S(2)}, u32[]{:S(2)}) collective-permute-start(bf16[1024,128]{1,0:T(8,128)(2,1)S(1)} %collective-permute-done.refs_0_), channel_id=1, source_target_pairs={{0,1},{1,0},{2,3},{3,2},{4,5},{5,4},{6,7},{7,6},{8,9},{9,8},{10,11... | collective-permute-start | bytes 786440 | tf_op jit(solution)/shard_map/ppermute | solution.py:145

commit v4 on v3

--- a/solution.py
+++ b/solution.py
@@ -12,7 +12,7 @@
 COLUMNS = 512
 
 
-def project_kernel(area_hbm, eofs_hbm, data_hbm, out_ref, area, eofs, scaled, data, sems):
+def project_kernel(weight_ref, area_hbm, eofs_hbm, data_hbm, out_ref, area, eofs, scaled, data, sems):
     pieces = data_hbm.shape[0] // ROWS
     weights = pltpu.make_async_copy(area_hbm, area, sems.at[pieces + 1])
     weights.start()
@@ -31,18 +31,18 @@
     for i in range(pieces):
         rows = pl.ds(i * ROWS, ROWS)
         loads[1 + i].wait()
-        out_ref[rows, :] = jnp.dot(
-            data[rows, :], scaled[...], preferred_element_type=jnp.float32
-        ).astype(jnp.bfloat16)
+        part = jnp.dot(data[rows, :], scaled[...], preferred_element_type=jnp.float32)
+        out_ref[rows, :] = (weight_ref[0] * part).astype(jnp.bfloat16)
 
 
-def project(area, eofs, data):
+def project(weight, area, eofs, data):
     steps, points = data.shape
     modes = eofs.shape[1]
     lanes = points // 128
     return pl.pallas_call(
         project_kernel,
         in_specs=[
+            pl.BlockSpec(memory_space=pltpu.SMEM),
             pl.BlockSpec(memory_space=pltpu.HBM),
             pl.BlockSpec(memory_space=pltpu.HBM),
             pl.BlockSpec(memory_space=pltpu.HBM),
@@ -58,6 +58,7 @@
         ],
         compiler_params=pltpu.CompilerParams(vmem_limit_bytes=32 << 20),
     )(
+        weight,
         pltpu.with_memory_space_constraint(area.reshape(lanes, 128), pltpu.HBM),
         pltpu.with_memory_space_constraint(eofs, pltpu.HBM),
         pltpu.with_memory_space_constraint(data, pltpu.HBM),
@@ -155,14 +156,14 @@
 
 
 def body(data, area, eofs, var_scale, recon_map):
-    partial_comps = project(area, eofs[0], data[0])
+    partial_comps = project(var_scale, area, eofs[0], data[0])
     patterns, partial_comps = lax.optimization_barrier((recon_map[0], partial_comps))
     steps, modes = partial_comps.shape
     points = lax.axis_size("z") * lax.axis_size("y")
     pieces = partial_comps.reshape(points, steps // points, modes)
     pieces = lax.all_to_all(pieces, GRID, 0, 0, tiled=True)
     comps = jnp.sum(pieces.astype(jnp.float32), axis=0)
-    own = (var_scale[0] * comps).astype(jnp.bfloat16)
+    own = lax.reduce_precision(comps, 8, 7).astype(jnp.bfloat16)
     spread = jnp.broadcast_to(own[None], (points, *own.shape))
     mine = lax.all_to_all(spread, GRID, 0, 0, tiled=True).reshape(steps, modes)
     return exchange_and_rebuild(mine, patterns)[None]

time: 63 us -> 62.9 us (level)
  blocking collectives: 15 us -> 38 us
  starting transfers between devices: 28.4 us -> 16.3 us
  waiting for transfers between devices: 10.6 us -> 0.02 us
  Pallas kernels: 8.07 us -> 7.39 us
    all_to_all x0 -> x1, blocking collectives: none -> 23 us  [body(): pieces = lax.all_to_all(pieces, GRID, 0, 0, tiled=True)]
    all_to_all x1 -> x0, starting transfers between devices: 12 us -> none  [body(): pieces = lax.all_to_all(pieces, GRID, 0, 0, tiled=True)]
    all_to_all x1 -> x0, waiting for transfers between devices: 10.5 us -> none  [body(): pieces = lax.all_to_all(pieces, GRID, 0, 0, tiled=True)]
    pallas_call x1, Pallas kernels: 3.62 us -> 2.93 us  [project(): pl.pallas_call(project_kernel, in_specs=[pl.BlockSpec(memory_space=pltpu....]
  transfers between devices with their start and end apart: 8 -> 7, of which waited for: 1 -> 0; matrix products, arithmetic and copies ran while one was open for 0% -> 0% of each run, Pallas kernels for 3% -> 3%
where the time goes in v4:
time: 62.9 us; the launch traced here: 62.7 us
  blocking collectives  38 us (60%)
  starting transfers between devices  16.3 us (26%)
  Pallas kernels  7.39 us (12%)
  between operations  0.86 us (1%)
    all_to_all x1, blocking collectives, body(): pieces = lax.all_to_all(pieces, GRID, 0, 0, tiled=True)  23 us
    ppermute x7, starting transfers between devices, shift(): lax.ppermute(block, axis, [(i, (i + by) % count) for i in range(count)])  16.3 us
    all_to_all x1, blocking collectives, body(): mine = lax.all_to_all(spread, GRID, 0, 0, tiled=True).reshape(steps, modes)  15 us
    pallas_call x1, Pallas kernels, project(): pl.pallas_call(project_kernel, in_specs=[pl.BlockSpec(memory_space=pltpu....  2.93 us
    pallas_call x1, Pallas kernels, finish(): pl.pallas_call(functools.partial(finish_kernel, sources), in_specs=[VMEM]...  2.65 us
    pallas_call x1, Pallas kernels, start(): pl.pallas_call(functools.partial(start_kernel, sources), in_specs=[VMEM]...  1.81 us
  transfers between devices with their start and end apart: 7, of which 0 were waited for; matrix products, arithmetic and copies ran while one was open for 0% of the time, Pallas kernels for 3%

profile of v4, /device:TPU:1, one launch (start us, length us, event | category | flops | bytes accessed | tf_op | source)
XLA Modules:
  0.0 62.7 jit_solution(1239439011379757754)
XLA Ops:
  0.0 0.0 copy-start
  0.8 2.9 %shard_map.55 = bf16[1024,128]{1,0:T(8,128)(2,1)S(1)} custom-call(f32[1]{0:T(128)S(6)} %copy.6.weight_ref, f32[12,128]{1,0:T(8,128)} %bitcast.17, bf16[1536,128]{1,0:T(8,128)(2,1)} %bitcast.16, bf16[1024,1536]{1,0:T(8,128)(2,1)} %bitcast.15), custom_call_target="tpu_custom_call" | custom-call | tf_op jit(solution)/shard_map/pallas_call | solution.py:42
  3.7 23.0 %all_to_all.10 = bf16[32,32,128]{2,1,0:T(8,128)(2,1)S(1)} all-to-all(bf16[32,32,128]{2,1,0:T(8,128)(2,1)S(1)} %bitcast.14), channel_id=1, replica_groups=mesh['z'=8,'y'=4,'x'=4,'c'=2] {'z','y'}, dimensions={0} | all-to-all | bytes 524288 | tf_op jit(solution)/shard_map/all_to_all | solution.py:164
  26.9 15.0 %all_to_all.11 = bf16[32,32,128]{2,1,0:T(8,128)(2,1)S(1)} all-to-all(bf16[32,32,128]{2,1,0:T(8,128)(2,1)S(1)} %broadcast_in_dim.4), channel_id=1, replica_groups=mesh['z'=8,'y'=4,'x'=4,'c'=2] {'z','y'}, dimensions={0} | all-to-all | bytes 524288 | tf_op jit(solution)/shard_map/all_to_all | solution.py:168
  41.8 2.7 %collective-permute-start.5 = (bf16[1024,128]{1,0:T(8,128)(2,1)S(1)}, bf16[1024,128]{1,0:T(8,128)(2,1)S(1)}, u32[]{:S(2)}, u32[]{:S(2)}) collective-permute-start(bf16[1024,128]{1,0:T(8,128)(2,1)S(1)} %bitcast.9), channel_id=1, source_target_pairs={{0,4},{2,6},{4,0},{6,2},{1,5},{3,7},{5,1},{7,3},{8,12},{10,14},{12... | collective-permute-start | bytes 786440 | tf_op jit(solution)/shard_map/ppermute | solution.py:146
  44.6 0.9 %collective-permute-start.2 = (bf16[1024,128]{1,0:T(8,128)(2,1)S(1)}, bf16[1024,128]{1,0:T(8,128)(2,1)S(1)}, u32[]{:S(2)}, u32[]{:S(2)}) collective-permute-start(bf16[1024,128]{1,0:T(8,128)(2,1)S(1)} %bitcast.10), channel_id=1, source_target_pairs={{0,6},{2,0},{4,2},{6,4},{1,7},{3,1},{5,3},{7,5},{8,14},{10,8},{12,... | collective-permute-start | bytes 786440 | tf_op jit(solution)/shard_map/ppermute | solution.py:146
  45.4 0.6 collective-permute-start
  46.0 4.6 %collective-permute-start.4 = (bf16[1024,128]{1,0:T(8,128)(2,1)S(1)}, bf16[1024,128]{1,0:T(8,128)(2,1)S(1)}, u32[]{:S(2)}, u32[]{:S(2)}) collective-permute-start(bf16[1024,128]{1,0:T(8,128)(2,1)S(1)} %bitcast.12), channel_id=1, source_target_pairs={{0,1},{1,0},{2,3},{3,2},{4,5},{5,4},{6,7},{7,6},{8,9},{9,8},{10,11... | collective-permute-start | bytes 786440 | tf_op jit(solution)/shard_map/ppermute | solution.py:146
  50.6 0.0 collective-permute-done.5.refs_2_
  50.6 4.3 %collective-permute-start.6 = (bf16[1024,128]{1,0:T(8,128)(2,1)S(1)}, bf16[1024,128]{1,0:T(8,128)(2,1)S(1)}, u32[]{:S(2)}, u32[]{:S(2)}) collective-permute-start(bf16[1024,128]{1,0:T(8,128)(2,1)S(1)} %collective-permute-done.5.refs_2_), channel_id=1, source_target_pairs={{0,1},{1,0},{2,3},{3,2},{4,5},{5,4},{6,7},{7,6},{8,9},{9,8},{10,11... | collective-permute-start | bytes 786440 | tf_op jit(solution)/shard_map/ppermute | solution.py:146
  55.0 0.0 collective-permute-done.2.refs_2_
  55.0 2.9 %collective-permute-start.3 = (bf16[1024,128]{1,0:T(8,128)(2,1)S(1)}, bf16[1024,128]{1,0:T(8,128)(2,1)S(1)}, u32[]{:S(2)}, u32[]{:S(2)}) collective-permute-start(bf16[1024,128]{1,0:T(8,128)(2,1)S(1)} %collective-permute-done.2.refs_2_), channel_id=1, source_target_pairs={{0,1},{1,0},{2,3},{3,2},{4,5},{5,4},{6,7},{7,6},{8,9},{9,8},{10,11... | collective-permute-start | bytes 786440 | tf_op jit(solution)/shard_map/ppermute | solution.py:146
  57.9 0.0 collective-permute-done.refs_0_
  57.9 0.3 collective-permute-start.1
  58.2 0.0 collective-permute-done.4.refs_1_
  58.2 0.0 collective-permute-done.6.refs_3_
  58.2 0.0 copy-done
  58.2 1.8 %shard_map.56.refs_5_ = f32[1024,1536]{1,0:T(8,128)S(1)} custom-call(bf16[1024,128]{1,0:T(8,128)(2,1)S(1)} %bitcast.13, bf16[1024,128]{1,0:T(8,128)(2,1)S(1)} %collective-permute-done.4.refs_1_, bf16[1024,128]{1,0:T(8,128)(2,1)S(1)} %collective-permute-done.5.refs_2_, bf16[1024,128]{1,0:T(8,128)(2,1)S(1)} %collective-permute-done.6.refs_3_, ...), custom_call_target="tpu_custom_call" | custom-call | tf_op jit(solution)/shard_map/pallas_call | solution.py:120
  60.0 0.0 collective-permute-done.3.refs_3_
  60.0 0.0 collective-permute-done.1.refs_1_
  60.0 2.7 %shard_map.57 = bf16[1024,1536]{1,0:T(8,128)(2,1)} custom-call(bf16[1024,128]{1,0:T(8,128)(2,1)S(1)} %collective-permute-done.refs_0_, bf16[1024,128]{1,0:T(8,128)(2,1)S(1)} %collective-permute-done.1.refs_1_, bf16[1024,128]{1,0:T(8,128)(2,1)S(1)} %collective-permute-done.2.refs_2_, bf16[1024,128]{1,0:T(8,128)(2,1)S(1)} %collective-permute-done.3.refs_3_, ...), custom_call_target="tpu_custom_call" | custom-call | tf_op jit(solution)/shard_map/pallas_call | solution.py:131
  (3 shorter events, 0.1 us)
Async XLA Ops:
  0.0 58.2 %copy-start = (bf16[1,1024,1536]{2,1,0:T(8,128)(2,1)S(1)}, bf16[1,1024,1536]{2,1,0:T(8,128)(2,1)}, u32[]{:S(2)}) copy-start(bf16[1,1024,1536]{2,1,0:T(8,128)(2,1)} %param.9) | copy-start | bytes 9437188
  41.8 8.8 %collective-permute-start.5 = (bf16[1024,128]{1,0:T(8,128)(2,1)S(1)}, bf16[1024,128]{1,0:T(8,128)(2,1)S(1)}, u32[]{:S(2)}, u32[]{:S(2)}) collective-permute-start(bf16[1024,128]{1,0:T(8,128)(2,1)S(1)} %bitcast.9), channel_id=1, source_target_pairs={{0,4},{2,6},{4,0},{6,2},{1,5},{3,7},{5,1},{7,3},{8,12},{10,14},{12... | collective-permute-start | bytes 786440 | tf_op jit(solution)/shard_map/ppermute | solution.py:146
  44.6 10.4 %collective-permute-start.2 = (bf16[1024,128]{1,0:T(8,128)(2,1)S(1)}, bf16[1024,128]{1,0:T(8,128)(2,1)S(1)}, u32[]{:S(2)}, u32[]{:S(2)}) collective-permute-start(bf16[1024,128]{1,0:T(8,128)(2,1)S(1)} %bitcast.10), channel_id=1, source_target_pairs={{0,6},{2,0},{4,2},{6,4},{1,7},{3,1},{5,3},{7,5},{8,14},{10,8},{12,... | collective-permute-start | bytes 786440 | tf_op jit(solution)/shard_map/ppermute | solution.py:146
  45.4 12.4 %collective-permute-start = (bf16[1024,128]{1,0:T(8,128)(2,1)S(1)}, bf16[1024,128]{1,0:T(8,128)(2,1)S(1)}, u32[]{:S(2)}, u32[]{:S(2)}) collective-permute-start(bf16[1024,128]{1,0:T(8,128)(2,1)S(1)} %bitcast.11), channel_id=1, source_target_pairs={{0,2},{2,4},{4,6},{6,0},{1,3},{3,5},{5,7},{7,1},{8,10},{10,12},{12... | collective-permute-start | bytes 786440 | tf_op jit(solution)/shard_map/ppermute | solution.py:146
  46.0 12.1 %collective-permute-start.4 = (bf16[1024,128]{1,0:T(8,128)(2,1)S(1)}, bf16[1024,128]{1,0:T(8,128)(2,1)S(1)}, u32[]{:S(2)}, u32[]{:S(2)}) collective-permute-start(bf16[1024,128]{1,0:T(8,128)(2,1)S(1)} %bitcast.12), channel_id=1, source_target_pairs={{0,1},{1,0},{2,3},{3,2},{4,5},{5,4},{6,7},{7,6},{8,9},{9,8},{10,11... | collective-permute-start | bytes 786440 | tf_op jit(solution)/shard_map/ppermute | solution.py:146
  50.6 7.5 %collective-permute-start.6 = (bf16[1024,128]{1,0:T(8,128)(2,1)S(1)}, bf16[1024,128]{1,0:T(8,128)(2,1)S(1)}, u32[]{:S(2)}, u32[]{:S(2)}) collective-permute-start(bf16[1024,128]{1,0:T(8,128)(2,1)S(1)} %collective-permute-done.5.refs_2_), channel_id=1, source_target_pairs={{0,1},{1,0},{2,3},{3,2},{4,5},{5,4},{6,7},{7,6},{8,9},{9,8},{10,11... | collective-permute-start | bytes 786440 | tf_op jit(solution)/shard_map/ppermute | solution.py:146
  55.0 5.0 %collective-permute-start.3 = (bf16[1024,128]{1,0:T(8,128)(2,1)S(1)}, bf16[1024,128]{1,0:T(8,128)(2,1)S(1)}, u32[]{:S(2)}, u32[]{:S(2)}) collective-permute-start(bf16[1024,128]{1,0:T(8,128)(2,1)S(1)} %collective-permute-done.2.refs_2_), channel_id=1, source_target_pairs={{0,1},{1,0},{2,3},{3,2},{4,5},{5,4},{6,7},{7,6},{8,9},{9,8},{10,11... | collective-permute-start | bytes 786440 | tf_op jit(solution)/shard_map/ppermute | solution.py:146
  57.9 2.2 %collective-permute-start.1 = (bf16[1024,128]{1,0:T(8,128)(2,1)S(1)}, bf16[1024,128]{1,0:T(8,128)(2,1)S(1)}, u32[]{:S(2)}, u32[]{:S(2)}) collective-permute-start(bf16[1024,128]{1,0:T(8,128)(2,1)S(1)} %collective-permute-done.refs_0_), channel_id=1, source_target_pairs={{0,1},{1,0},{2,3},{3,2},{4,5},{5,4},{6,7},{7,6},{8,9},{9,8},{10,11... | collective-permute-start | bytes 786440 | tf_op jit(solution)/shard_map/ppermute | solution.py:146

commit v5 on v4

--- a/solution.py
+++ b/solution.py
@@ -86,16 +86,15 @@
 
 
 def start_kernel(sources, *refs):
-    blocks, patterns_ref, total_ref = refs[:-2], refs[-2], refs[-1]
-    steps, points = total_ref.shape
+    blocks, patterns_ref, totals = refs[: 2 * len(sources)], refs[2 * len(sources)], refs[2 * len(sources) + 1 :]
+    steps, points = totals[-1].shape
     joined, patterns = operands(blocks, sources, patterns_ref)
     for i in range(steps // ROWS):
         rows = pl.ds(i * ROWS, ROWS)
         for j in range(points // COLUMNS):
             columns = pl.ds(j * COLUMNS, COLUMNS)
-            total_ref[rows, columns] = jnp.dot(
-                joined(rows), patterns(columns), preferred_element_type=jnp.float32
-            )
+            part = jnp.dot(joined(rows), patterns(columns), preferred_element_type=jnp.float32)
+            totals[-1][rows, columns] = totals[0][rows, columns] + part if len(totals) > 1 else part
 
 
 def finish_kernel(sources, *refs):
@@ -115,15 +114,16 @@
         store.wait()
 
 
-def start(blocks, sources, patterns):
+def start(blocks, sources, patterns, total=()):
     steps, points = blocks[0].shape[0], patterns.shape[1]
     return pl.pallas_call(
         functools.partial(start_kernel, sources),
-        in_specs=[VMEM] * (len(blocks) + 1),
+        in_specs=[VMEM] * (len(blocks) + 1 + len(total)),
         out_specs=VMEM,
         out_shape=pltpu.VMEM((steps, points), jnp.float32),
+        input_output_aliases={len(blocks) + 1: 0} if total else {},
         compiler_params=pltpu.CompilerParams(vmem_limit_bytes=16 << 20),
-    )(*blocks, patterns)
+    )(*blocks, patterns, *total)
 
 
 def finish(blocks, sources, patterns, total):
@@ -147,11 +147,10 @@
 
 
 def exchange_and_rebuild(mine, patterns):
-    blocks = [mine, shift(mine, "x", 2), shift(mine, "x", 1), shift(mine, "x", 3)]
-    blocks = [(block, shift(block, "c", 1)) for block in blocks]
-    early = [part for pair in blocks[:2] for part in pair]
-    late = [part for pair in blocks[2:] for part in pair]
-    total = start(early, (0, 2), patterns)
+    far, left, right = shift(mine, "x", 2), shift(mine, "x", 1), shift(mine, "x", 3)
+    total = start([mine, shift(mine, "c", 1)], (0,), patterns)
+    total = start([far, shift(far, "c", 1)], (2,), patterns, (total,))
+    late = [left, shift(left, "c", 1), right, shift(right, "c", 1)]
     return finish(late, (3, 1), patterns, total)
 
 

time: 62.9 us -> 62.9 us (level)
    pallas_call x1 -> x2, Pallas kernels: 1.81 us -> 2.2 us  [start(): pl.pallas_call(functools.partial(start_kernel, sources), in_specs=[VMEM]...]
  transfers between devices with their start and end apart: 7 -> 7, of which waited for: 0 -> 0; matrix products, arithmetic and copies ran while one was open for 0% -> 0% of each run, Pallas kernels for 3% -> 4%
where the time goes in v5:
time: 62.9 us; the launch traced here: 62.7 us
  blocking collectives  38 us (60%)
  starting transfers between devices  15.9 us (25%)
  Pallas kernels  7.78 us (12%)
  between operations  0.87 us (1%)
    all_to_all x1, blocking collectives, body(): pieces = lax.all_to_all(pieces, GRID, 0, 0, tiled=True)  23 us
    ppermute x7, starting transfers between devices, shift(): lax.ppermute(block, axis, [(i, (i + by) % count) for i in range(count)])  15.9 us
    all_to_all x1, blocking collectives, body(): mine = lax.all_to_all(spread, GRID, 0, 0, tiled=True).reshape(steps, modes)  15 us
    pallas_call x1, Pallas kernels, project(): pl.pallas_call(project_kernel, in_specs=[pl.BlockSpec(memory_space=pltpu....  2.93 us
    pallas_call x1, Pallas kernels, finish(): pl.pallas_call(functools.partial(finish_kernel, sources), in_specs=[VMEM]...  2.65 us
    pallas_call x2, Pallas kernels, start(): pl.pallas_call(functools.partial(start_kernel, sources), in_specs=[VMEM]...  2.2 us
  transfers between devices with their start and end apart: 7, of which 0 were waited for; matrix products, arithmetic and copies ran while one was open for 0% of the time, Pallas kernels for 4%

profile of v5, /device:TPU:1, one launch (start us, length us, event | category | flops | bytes accessed | tf_op | source)
XLA Modules:
  0.0 62.7 jit_solution(11259621781342459983)
XLA Ops:
  0.0 0.0 copy-start
  0.8 2.9 %shard_map.55 = bf16[1024,128]{1,0:T(8,128)(2,1)S(1)} custom-call(f32[1]{0:T(128)S(6)} %copy.8.weight_ref, f32[12,128]{1,0:T(8,128)} %bitcast.18, bf16[1536,128]{1,0:T(8,128)(2,1)} %bitcast.17, bf16[1024,1536]{1,0:T(8,128)(2,1)} %bitcast.16), custom_call_target="tpu_custom_call" | custom-call | tf_op jit(solution)/shard_map/pallas_call | solution.py:42
  3.7 23.0 %all_to_all.10 = bf16[32,32,128]{2,1,0:T(8,128)(2,1)S(1)} all-to-all(bf16[32,32,128]{2,1,0:T(8,128)(2,1)S(1)} %bitcast.15), channel_id=1, replica_groups=mesh['z'=8,'y'=4,'x'=4,'c'=2] {'z','y'}, dimensions={0} | all-to-all | bytes 524288 | tf_op jit(solution)/shard_map/all_to_all | solution.py:163
  26.9 15.0 %all_to_all.11 = bf16[32,32,128]{2,1,0:T(8,128)(2,1)S(1)} all-to-all(bf16[32,32,128]{2,1,0:T(8,128)(2,1)S(1)} %broadcast_in_dim.4), channel_id=1, replica_groups=mesh['z'=8,'y'=4,'x'=4,'c'=2] {'z','y'}, dimensions={0} | all-to-all | bytes 524288 | tf_op jit(solution)/shard_map/all_to_all | solution.py:167
  41.8 2.7 %collective-permute-start.4 = (bf16[1024,128]{1,0:T(8,128)(2,1)S(1)}, bf16[1024,128]{1,0:T(8,128)(2,1)S(1)}, u32[]{:S(2)}, u32[]{:S(2)}) collective-permute-start(bf16[1024,128]{1,0:T(8,128)(2,1)S(1)} %bitcast.10), channel_id=1, source_target_pairs={{0,4},{2,6},{4,0},{6,2},{1,5},{3,7},{5,1},{7,3},{8,12},{10,14},{12... | collective-permute-start | bytes 786440 | tf_op jit(solution)/shard_map/ppermute | solution.py:146
  44.6 0.3 collective-permute-start
  44.9 2.4 %collective-permute-start.2 = (bf16[1024,128]{1,0:T(8,128)(2,1)S(1)}, bf16[1024,128]{1,0:T(8,128)(2,1)S(1)}, u32[]{:S(2)}, u32[]{:S(2)}) collective-permute-start(bf16[1024,128]{1,0:T(8,128)(2,1)S(1)} %bitcast.12), channel_id=1, source_target_pairs={{0,6},{2,0},{4,2},{6,4},{1,7},{3,1},{5,3},{7,5},{8,14},{10,8},{12,... | collective-permute-start | bytes 786440 | tf_op jit(solution)/shard_map/ppermute | solution.py:146
  47.3 4.6 %collective-permute-start.6 = (bf16[1024,128]{1,0:T(8,128)(2,1)S(1)}, bf16[1024,128]{1,0:T(8,128)(2,1)S(1)}, u32[]{:S(2)}, u32[]{:S(2)}) collective-permute-start(bf16[1024,128]{1,0:T(8,128)(2,1)S(1)} %bitcast.13), channel_id=1, source_target_pairs={{0,1},{1,0},{2,3},{3,2},{4,5},{5,4},{6,7},{7,6},{8,9},{9,8},{10,11... | collective-permute-start | bytes 786440 | tf_op jit(solution)/shard_map/ppermute | solution.py:146
  51.9 0.0 collective-permute-done.4.refs_0_
  51.9 3.1 %collective-permute-start.5 = (bf16[1024,128]{1,0:T(8,128)(2,1)S(1)}, bf16[1024,128]{1,0:T(8,128)(2,1)S(1)}, u32[]{:S(2)}, u32[]{:S(2)}) collective-permute-start(bf16[1024,128]{1,0:T(8,128)(2,1)S(1)} %collective-permute-done.4.refs_0_), channel_id=1, source_target_pairs={{0,1},{1,0},{2,3},{3,2},{4,5},{5,4},{6,7},{7,6},{8,9},{9,8},{10,11... | collective-permute-start | bytes 786440 | tf_op jit(solution)/shard_map/ppermute | solution.py:146
  55.0 0.0 collective-permute-done.refs_0_
  55.0 2.7 %collective-permute-start.1 = (bf16[1024,128]{1,0:T(8,128)(2,1)S(1)}, bf16[1024,128]{1,0:T(8,128)(2,1)S(1)}, u32[]{:S(2)}, u32[]{:S(2)}) collective-permute-start(bf16[1024,128]{1,0:T(8,128)(2,1)S(1)} %collective-permute-done.refs_0_), channel_id=1, source_target_pairs={{0,1},{1,0},{2,3},{3,2},{4,5},{5,4},{6,7},{7,6},{8,9},{9,8},{10,11... | collective-permute-start | bytes 786440 | tf_op jit(solution)/shard_map/ppermute | solution.py:146
  57.7 0.0 collective-permute-done.2.refs_2_
  57.7 0.1 collective-permute-start.3
  57.8 0.0 collective-permute-done.6.refs_1_
  57.8 0.0 copy-done
  57.8 1.0 %shard_map.56.refs_3_ = f32[1024,1536]{1,0:T(8,128)S(1)} custom-call(bf16[1024,128]{1,0:T(8,128)(2,1)S(1)} %bitcast.14, bf16[1024,128]{1,0:T(8,128)(2,1)S(1)} %collective-permute-done.6.refs_1_, bf16[1024,1536]{1,0:T(8,128)(2,1)S(1)} %bitcast.7), custom_call_target="tpu_custom_call" | custom-call | tf_op jit(solution)/shard_map/pallas_call | solution.py:119
  58.8 0.0 collective-permute-done.5.refs_1_
  58.8 1.2 %shard_map.57.refs_5_ = f32[1024,1536]{1,0:T(8,128)S(1)} custom-call(bf16[1024,128]{1,0:T(8,128)(2,1)S(1)} %collective-permute-done.4.refs_0_, bf16[1024,128]{1,0:T(8,128)(2,1)S(1)} %collective-permute-done.5.refs_1_, bf16[1024,1536]{1,0:T(8,128)(2,1)S(1)} %bitcast.8, f32[1024,1536]{1,0:T(8,128)S(1)} %shard_map.56.refs_3_), custom_call_target="tpu_custom_call", output_to_operand_aliasing={{}: (3, {})} | custom-call | tf_op jit(solution)/shard_map/pallas_call | solution.py:119
  60.0 0.0 collective-permute-done.1.refs_1_
  60.0 0.0 collective-permute-done.3.refs_3_
  60.0 2.6 %shard_map.58 = bf16[1024,1536]{1,0:T(8,128)(2,1)} custom-call(bf16[1024,128]{1,0:T(8,128)(2,1)S(1)} %collective-permute-done.refs_0_, bf16[1024,128]{1,0:T(8,128)(2,1)S(1)} %collective-permute-done.1.refs_1_, bf16[1024,128]{1,0:T(8,128)(2,1)S(1)} %collective-permute-done.2.refs_2_, bf16[1024,128]{1,0:T(8,128)(2,1)S(1)} %collective-permute-done.3.refs_3_, ...), custom_call_target="tpu_custom_call" | custom-call | tf_op jit(solution)/shard_map/pallas_call | solution.py:131
  (3 shorter events, 0.1 us)
Async XLA Ops:
  0.0 57.8 %copy-start = (bf16[1,1024,1536]{2,1,0:T(8,128)(2,1)S(1)}, bf16[1,1024,1536]{2,1,0:T(8,128)(2,1)}, u32[]{:S(2)}) copy-start(bf16[1,1024,1536]{2,1,0:T(8,128)(2,1)} %param.9) | copy-start | bytes 9437188
  41.8 10.0 %collective-permute-start.4 = (bf16[1024,128]{1,0:T(8,128)(2,1)S(1)}, bf16[1024,128]{1,0:T(8,128)(2,1)S(1)}, u32[]{:S(2)}, u32[]{:S(2)}) collective-permute-start(bf16[1024,128]{1,0:T(8,128)(2,1)S(1)} %bitcast.10), channel_id=1, source_target_pairs={{0,4},{2,6},{4,0},{6,2},{1,5},{3,7},{5,1},{7,3},{8,12},{10,14},{12... | collective-permute-start | bytes 786440 | tf_op jit(solution)/shard_map/ppermute | solution.py:146
  44.6 10.4 %collective-permute-start = (bf16[1024,128]{1,0:T(8,128)(2,1)S(1)}, bf16[1024,128]{1,0:T(8,128)(2,1)S(1)}, u32[]{:S(2)}, u32[]{:S(2)}) collective-permute-start(bf16[1024,128]{1,0:T(8,128)(2,1)S(1)} %bitcast.11), channel_id=1, source_target_pairs={{0,2},{2,4},{4,6},{6,0},{1,3},{3,5},{5,7},{7,1},{8,10},{10,12},{12... | collective-permute-start | bytes 786440 | tf_op jit(solution)/shard_map/ppermute | solution.py:146
  44.9 12.8 %collective-permute-start.2 = (bf16[1024,128]{1,0:T(8,128)(2,1)S(1)}, bf16[1024,128]{1,0:T(8,128)(2,1)S(1)}, u32[]{:S(2)}, u32[]{:S(2)}) collective-permute-start(bf16[1024,128]{1,0:T(8,128)(2,1)S(1)} %bitcast.12), channel_id=1, source_target_pairs={{0,6},{2,0},{4,2},{6,4},{1,7},{3,1},{5,3},{7,5},{8,14},{10,8},{12,... | collective-permute-start | bytes 786440 | tf_op jit(solution)/shard_map/ppermute | solution.py:146
  47.3 10.5 %collective-permute-start.6 = (bf16[1024,128]{1,0:T(8,128)(2,1)S(1)}, bf16[1024,128]{1,0:T(8,128)(2,1)S(1)}, u32[]{:S(2)}, u32[]{:S(2)}) collective-permute-start(bf16[1024,128]{1,0:T(8,128)(2,1)S(1)} %bitcast.13), channel_id=1, source_target_pairs={{0,1},{1,0},{2,3},{3,2},{4,5},{5,4},{6,7},{7,6},{8,9},{9,8},{10,11... | collective-permute-start | bytes 786440 | tf_op jit(solution)/shard_map/ppermute | solution.py:146
  51.9 6.9 %collective-permute-start.5 = (bf16[1024,128]{1,0:T(8,128)(2,1)S(1)}, bf16[1024,128]{1,0:T(8,128)(2,1)S(1)}, u32[]{:S(2)}, u32[]{:S(2)}) collective-permute-start(bf16[1024,128]{1,0:T(8,128)(2,1)S(1)} %collective-permute-done.4.refs_0_), channel_id=1, source_target_pairs={{0,1},{1,0},{2,3},{3,2},{4,5},{5,4},{6,7},{7,6},{8,9},{9,8},{10,11... | collective-permute-start | bytes 786440 | tf_op jit(solution)/shard_map/ppermute | solution.py:146
  55.0 5.0 %collective-permute-start.1 = (bf16[1024,128]{1,0:T(8,128)(2,1)S(1)}, bf16[1024,128]{1,0:T(8,128)(2,1)S(1)}, u32[]{:S(2)}, u32[]{:S(2)}) collective-permute-start(bf16[1024,128]{1,0:T(8,128)(2,1)S(1)} %collective-permute-done.refs_0_), channel_id=1, source_target_pairs={{0,1},{1,0},{2,3},{3,2},{4,5},{5,4},{6,7},{7,6},{8,9},{9,8},{10,11... | collective-permute-start | bytes 786440 | tf_op jit(solution)/shard_map/ppermute | solution.py:146
  57.7 2.3 %collective-permute-start.3 = (bf16[1024,128]{1,0:T(8,128)(2,1)S(1)}, bf16[1024,128]{1,0:T(8,128)(2,1)S(1)}, u32[]{:S(2)}, u32[]{:S(2)}) collective-permute-start(bf16[1024,128]{1,0:T(8,128)(2,1)S(1)} %collective-permute-done.2.refs_2_), channel_id=1, source_target_pairs={{0,1},{1,0},{2,3},{3,2},{4,5},{5,4},{6,7},{7,6},{8,9},{9,8},{10,11... | collective-permute-start | bytes 786440 | tf_op jit(solution)/shard_map/ppermute | solution.py:146
